TPU v7x, 256 devices: a whole 4x4x8 slice. The times are simulated.
256 devices in a mesh: tile: 128 (over z_hi, x, y, core), member: 2 (over z_lo).
Axes of the slice: x: 4, y: 4, z: 8 (z_hi: 4, z_lo: 2; z = z_hi * 2 + z_lo), core: 2. Of those that a mesh axis runs over, the one named last changes fastest.
Arguments:
- fields: bfloat16 [2, 128, 2, 32, 32, 128], P('member', 'tile'), may hold values from -6 to 6
- cotangent: bfloat16 [2, 128, 2, 32, 32, 128], P('member', 'tile'), may hold values from -6 to 6
- edge_map: int32 [128, 4, 2], P('tile'), may hold values from 0 to 3, as said below
- w_first: bfloat16 [3, 3, 128, 128], replicated, may hold values from -0.1875 to 0.1875
- b_first: float32 [128], replicated, may hold values from -3 to 3
- w_second: bfloat16 [3, 3, 128, 128], replicated, may hold values from -0.1875 to 0.1875
- b_second: float32 [128], replicated, may hold values from -3 to 3
Outputs:
- response: bfloat16 [2, 128, 2, 32, 32, 128], P('member', 'tile')
- field_grad: bfloat16 [2, 128, 2, 32, 32, 128], P('member', 'tile')
- first_kernel_grad: float32 [3, 3, 128, 128], replicated
- first_bias_grad: float32 [128], replicated
- second_kernel_grad: float32 [3, 3, 128, 128], replicated
- second_bias_grad: float32 [128], replicated
Inputs may be any that keep to these rules, and one draw needn't show every extreme that they name: Each tile t is its own grid turned by r quarter turns: edge_map[t, g, 0] = (g - r) mod 4, and edge_map[t, g, 1] is 1 exactly when r = 2, or r = 1 and g is even, or r = 3 and g is odd.
All inputs are finite; a program needn't handle non-finite values.
Results may differ from a plain program's by a relative error of at most 0.0065.
Values may be sent and summed in bfloat16 or wider, within the bound.
A program may use at most 64 MiB of HBM per device.

v0:
```python
import functools

import jax
import jax.numpy as jnp
from jax import lax
from jax.experimental import pallas as pl
from jax.experimental.pallas import tpu as pltpu
from jax.sharding import PartitionSpec as P

ROW_TILES = 8
ROOT_HALF = 0.7071067811865476
INV_ROOT_TAU = 0.3989422804014327
BF16 = jnp.bfloat16
F32 = jnp.float32

PLANE = 16
DEPTH = 8
PIECE = 5
HALF = PLANE * PIECE
PART_ROWS = 2 * HALF * 8


def coordinates():
    tile = lax.axis_index("tile")
    member = lax.axis_index("member")
    core = lax.rem(tile, 2)
    spot = lax.rem(tile // 2, PLANE)
    floor = tile // (2 * PLANE)
    return tile, member, core, spot, floor


def sum_partners():
    tile, member, core, spot, floor = coordinates()
    mate = (tile - core + (1 - core), member)
    plane = [
        ((floor * PLANE + lax.rem(spot + step, PLANE)) * 2 + core, member)
        for step in range(1, PLANE)
    ]
    level = floor * 2 + member
    column = []
    for step in range(1, DEPTH):
        other = lax.rem(level + step, DEPTH)
        column.append((((other // 2) * PLANE + spot) * 2 + core, lax.rem(other, 2)))
    return mate, plane, column


def remote(source, target, send_sem, recv_sem, device):
    return pltpu.make_async_remote_copy(
        src_ref=source,
        dst_ref=target,
        send_sem=send_sem,
        recv_sem=recv_sem,
        device_id=device,
        device_id_type=pl.DeviceIdType.MESH,
    )


def sum_scratch():
    dma = pltpu.SemaphoreType.DMA
    return [
        pltpu.VMEM((2 * HALF, 8, 128), jnp.float32),
        pltpu.VMEM((2 * HALF, 8, 128), jnp.bfloat16),
        pltpu.VMEM((HALF, 8, 128), jnp.bfloat16),
        pltpu.VMEM((PLANE, PIECE, 8, 128), jnp.float32),
        pltpu.VMEM((PLANE, PIECE, 8, 128), jnp.bfloat16),
        pltpu.VMEM((PLANE, PIECE, 8, 128), jnp.bfloat16),
        pltpu.VMEM((DEPTH, PIECE, 8, 128), jnp.bfloat16),
        pltpu.VMEM((2, PLANE, PIECE, 8, 128), jnp.bfloat16),
        dma((2,)),
        dma((2, PLANE)),
        dma((2, DEPTH)),
        dma((2, PLANE)),
        dma((2, PLANE)),
    ]


class GradientSum:
    def __init__(self, refs):
        (
            self.own,
            self.halves,
            self.from_mate,
            self.total,
            self.pieces,
            self.from_plane,
            self.from_column,
            self.gathered,
            self.mate_sem,
            self.plane_sem,
            self.column_sem,
            self.gather_sem,
            self.forward_sem,
        ) = refs
        tile, member, core, spot, floor = coordinates()
        self.core, self.spot, self.level = core, spot, floor * 2 + member
        self.mate, self.plane, self.column = sum_partners()

    def to_mate(self):
        return remote(
            self.halves.at[pl.ds((1 - self.core) * HALF, HALF)],
            self.from_mate,
            self.mate_sem.at[0],
            self.mate_sem.at[1],
            self.mate,
        )

    def to_plane(self, step):
        target = lax.rem(self.spot + step, PLANE)
        return remote(
            self.pieces.at[target],
            self.from_plane.at[self.spot],
            self.plane_sem.at[0, step],
            self.plane_sem.at[1, step],
            self.plane[step - 1],
        )

    def to_column(self, step):
        return remote(
            self.from_column.at[self.level],
            self.from_column.at[self.level],
            self.column_sem.at[0, step],
            self.column_sem.at[1, step],
            self.column[step - 1],
        )

    def to_gather(self, step):
        return remote(
            self.gathered.at[self.core, self.spot],
            self.gathered.at[self.core, self.spot],
            self.gather_sem.at[0, step],
            self.gather_sem.at[1, step],
            self.plane[step - 1],
        )

    def to_forward(self, step):
        origin = lax.rem(self.spot + PLANE - step, PLANE)
        return remote(
            self.gathered.at[self.core, origin],
            self.gathered.at[self.core, origin],
            self.forward_sem.at[0, step],
            self.forward_sem.at[1, step],
            self.mate,
        )

    def start(self):
        self.halves[...] = self.own[...].astype(jnp.bfloat16)
        self.to_mate().start()

    def spread_plane(self):
        self.to_mate().wait_recv()
        total = self.own[pl.ds(self.core * HALF, HALF)] + self.from_mate[...].astype(jnp.float32)
        total = total.reshape(PLANE, PIECE, 8, 128)
        self.total[...] = total
        self.pieces[...] = total.astype(jnp.bfloat16)
        for step in range(1, PLANE):
            self.to_plane(step).start()

    def spread_column(self):
        value = self.total[self.spot]
        for step in range(1, PLANE):
            self.to_plane(step).wait_recv()
            origin = lax.rem(self.spot + PLANE - step, PLANE)
            value = value + self.from_plane[origin].astype(jnp.float32)
        self.from_column[self.level] = value.astype(jnp.bfloat16)
        for step in range(1, DEPTH):
            self.to_column(step).start()

    def gather_plane(self):
        for step in range(1, DEPTH):
            self.to_column(step).wait_recv()
        value = jnp.zeros((PIECE, 8, 128), jnp.float32)
        for level in range(DEPTH):
            value = value + self.from_column[level].astype(jnp.float32)
        self.gathered[self.core, self.spot] = value.astype(jnp.bfloat16)
        for step in range(1, PLANE):
            self.to_gather(step).start()
        self.to_forward(0).start()

    def forward(self):
        for step in range(1, PLANE):
            self.to_gather(step).wait_recv()
            self.to_forward(step).start()

    def finish(self):
        for step in range(PLANE):
            self.to_forward(step).wait_recv()

    def drain(self):
        self.to_mate().wait_send()
        for step in range(1, PLANE):
            self.to_plane(step).wait_send()
            self.to_gather(step).wait_send()
        for step in range(1, DEPTH):
            self.to_column(step).wait_send()
        for step in range(PLANE):
            self.to_forward(step).wait_send()


def dot(left, right):
    return jnp.dot(left, right, preferred_element_type=F32)


def dot_nt(left, right):
    return lax.dot_general(left, right, (((1,), (1,)), ((), ())), preferred_element_type=F32)


def dot_tn(left, right):
    return lax.dot_general(left, right, (((0,), (0,)), ((), ())), preferred_element_type=F32)


def iota(shape, axis):
    return lax.broadcasted_iota(jnp.int32, shape, axis)


def ones_where(mask):
    return jnp.where(mask, 1.0, 0.0).astype(BF16)


def border_pixel(side, place):
    return jnp.where(
        side == 0,
        place,
        jnp.where(side == 1, place * 32 + 31, jnp.where(side == 2, place + 992, place * 32)),
    )


def facing(edge_map, index):
    direction, place = index >> 5, index & 31
    side = jnp.zeros_like(index)
    flip = jnp.zeros_like(index)
    for candidate in range(4):
        side = jnp.where(direction == candidate, edge_map[candidate, 0], side)
        flip = jnp.where(direction == candidate, edge_map[candidate, 1], flip)
    return side, jnp.where(flip == 1, 31 - place, place)


def ring_taps(tap):
    row, lane = iota((128, 128), 0), iota((128, 128), 1)
    side, place = row >> 5, row & 31
    halo_side, halo_place = lane >> 5, lane & 31
    wanted = place + (tap - 1)
    whole = (halo_side == side) & (halo_place == wanted)
    along = (side == 0) | (side == 2)
    end = jnp.where(side == 0, 0, 31)
    low = ((halo_side == side) & (halo_place == 0)) | ((halo_side == 3) & (halo_place == end))
    high = ((halo_side == side) & (halo_place == 31)) | ((halo_side == 1) & (halo_place == end))
    half = along & (((wanted == -1) & low) | ((wanted == 32) & high))
    return jnp.where(whole, 1.0, jnp.where(half, 0.5, 0.0)).astype(BF16)


def side_tap(side, tap):
    return ((0, tap), (tap, 2), (2, tap), (tap, 0))[side]


def split_float(value):
    high = value.astype(BF16)
    low = (value - high.astype(F32)).astype(BF16)
    return jnp.concatenate([high, low], axis=0)


def make_tables(edge_map, t):
    row, lane = iota((128, 128), 0), iota((128, 128), 1)
    side, place = facing(edge_map, row)
    pixel = border_pixel(side, place)
    plain = border_pixel(row >> 5, row & 31)
    turn = ones_where(lane == side * 32 + place)
    for block in range(8):
        here = lane + block * 128
        t.pick[:, block * 128 : (block + 1) * 128] = ones_where(here == pixel)
        t.border[:, block * 128 : (block + 1) * 128] = ones_where(here == plain)
    lane_side, lane_place = facing(edge_map, lane)
    lane_pixel = border_pixel(lane_side, lane_place)
    lane_plain = border_pixel(lane >> 5, lane & 31)
    for block in range(8):
        here = row + block * 128
        rows = slice(block * 128, (block + 1) * 128)
        t.put_in[rows, :] = ones_where(here == lane_pixel)
        marks = ones_where(here == lane_plain)
        t.put[rows, 0:128] = marks
        t.put[rows, 128:256] = marks
    for tap in range(3):
        taps = ring_taps(tap)
        t.ring[tap * 128 : (tap + 1) * 128, :] = dot_nt(taps, turn).astype(BF16)
        back = dot_nt(turn, taps).astype(BF16)
        t.ring_back[:, tap * 128 : (tap + 1) * 128] = back
        t.ring_back[:, 384 + tap * 128 : 384 + (tap + 1) * 128] = back


def lay_weights(target, block):
    empty = jnp.zeros((384, 128), BF16)
    target[0, :, 128:256] = empty
    target[3, :, 0:128] = empty
    for row in range(3):
        for col in range(3):
            part = block(row, col)
            target[row, col * 128 : (col + 1) * 128, 0:128] = part
            target[row + 1, col * 128 : (col + 1) * 128, 128:256] = part


def lay_shifted(target, frame, pair, value):
    col = iota((64, 128), 0) & 31
    before = jnp.where(col == 0, 0.0, pltpu.roll(value, 1, 0))
    after = jnp.where(col == 31, 0.0, pltpu.roll(value, 63, 0))
    for tap, part in enumerate((before, value, after)):
        target[frame, pl.ds(1 + 2 * pair, 2), :, tap * 128 : (tap + 1) * 128] = part.astype(
            BF16
        ).reshape(2, 32, 128)


def lay_rows(target, frame, pair, value):
    part = value.reshape(2, 32, 128)
    for tap in range(3):
        target[frame, pl.ds(2 * pair + tap, 2), :, tap * 128 : (tap + 1) * 128] = part


def clear_rims(shifted):
    for frame in range(2):
        shifted[frame, 0] = jnp.zeros((32, 384), BF16)
        shifted[frame, 33] = jnp.zeros((32, 384), BF16)
        shifted[frame, 34] = jnp.zeros((32, 384), BF16)


def tile_conv(shifted, weights, result):
    for frame in range(2):
        total = None
        for row in range(4):
            rows = shifted[frame, row : row + 32].reshape(16, 2, 32, 384)[:, 0].reshape(512, 384)
            part = dot(rows, weights[row])
            total = part if total is None else total + part
        pairs = slice(frame * 16, (frame + 1) * 16)
        result[pairs, 0:32, :] = total[:, 0:128].reshape(16, 32, 128)
        result[pairs, 32:64, :] = total[:, 128:256].reshape(16, 32, 128)


def transpose_shifted(shifted, target):
    for frame in range(2):
        for tap in range(3):
            lanes = slice(tap * 128, (tap + 1) * 128)
            target[lanes, frame * 1024 : (frame + 1) * 1024] = (
                shifted[frame, 1:33, :, lanes].reshape(1024, 128).T
            )


def picked(table, image):
    parts = [
        dot(table[...], image[frame * 16 : (frame + 1) * 16].reshape(1024, 128))
        for frame in range(2)
    ]
    return jnp.concatenate(parts, axis=1).astype(BF16)


def halo_share(t, arrived, weights, ring_rows, share):
    around = dot(t.ring[...], arrived[...].reshape(128, 256)).astype(BF16)
    parts = []
    for side in range(4):
        for frame in range(2):
            lanes = slice(frame * 128, (frame + 1) * 128)
            ring_rows[side, frame * 32 : (frame + 1) * 32, :] = jnp.concatenate(
                [
                    around[tap * 128 + side * 32 : tap * 128 + (side + 1) * 32, lanes]
                    for tap in range(3)
                ],
                axis=1,
            )
        taps = jnp.concatenate([weights[side_tap(side, tap)] for tap in range(3)], axis=0)
        value = dot(ring_rows[side], taps)
        parts.append(jnp.concatenate([value[0:32], value[32:64]], axis=1))
    both = split_float(jnp.concatenate(parts, axis=0))
    share[...] = dot(t.put[...], both).reshape(16, 64, 256)


def ring_gradient(t, image, weights, border_rows, leaving):
    border = picked(t.border, image)
    rows = [[None] * 4 for tap in range(3)]
    for side in range(4):
        here = border[side * 32 : (side + 1) * 32]
        border_rows[side] = jnp.concatenate([here[:, 0:128], here[:, 128:256]], axis=0)
        for tap in range(3):
            value = dot_nt(border_rows[side], weights[side_tap(side, tap)])
            rows[tap][side] = jnp.concatenate([value[0:32], value[32:64]], axis=1)
    stacked = jnp.concatenate([rows[tap][side] for tap in range(3) for side in range(4)], axis=0)
    leaving[...] = dot(t.ring_back[...], split_float(stacked)).astype(BF16).reshape(4, 32, 256)


def kernel_gradient(turned, spread_rows, ring_rows, border_rows, bias, block, own):
    total = None
    for frame in range(2):
        part = dot(
            turned[:, frame * 1024 : (frame + 1) * 1024],
            spread_rows[frame, 1:33].reshape(1024, 384),
        )
        total = part if total is None else total + part
    block[...] = total
    for side in range(4):
        part = dot_tn(ring_rows[side], border_rows[side])
        for tap in range(3):
            row, col = side_tap(side, tap)
            at = (slice(col * 128, (col + 1) * 128), slice(row * 128, (row + 1) * 128))
            block[at] += part[tap * 128 : (tap + 1) * 128]
    for row in range(3):
        for col in range(3):
            first = (row * 3 + col) * 16
            own[first : first + 16] = block[
                col * 128 : (col + 1) * 128, row * 128 : (row + 1) * 128
            ].reshape(16, 8, 128)
    own[144] = jnp.concatenate([bias, jnp.zeros((7, 128), F32)], axis=0)
    own[145:160] = jnp.zeros((15, 8, 128), F32)


def halo_partners():
    tile, member, core, spot, floor = coordinates()
    count = 2 * PLANE * (DEPTH // 2)
    steps = (count - ROW_TILES, 1, ROW_TILES, count - 1)
    return [(lax.rem(tile + step, count), member) for step in steps]


class Halo:
    def __init__(self, leaving, arrived, send_sem, recv_sem):
        self.leaving, self.arrived = leaving, arrived
        self.send_sem, self.recv_sem = send_sem, recv_sem
        self.partners = halo_partners()

    def copies(self, turn):
        return [
            remote(
                self.leaving.at[turn, way],
                self.arrived.at[turn, (way + 2) % 4],
                self.send_sem.at[turn, way],
                self.recv_sem.at[turn, (way + 2) % 4],
                self.partners[way],
            )
            for way in range(4)
        ]

    def start(self, turn):
        for copy in self.copies(turn):
            copy.start()

    def wait(self, turn):
        for copy in self.copies(turn):
            copy.wait_recv()

    def drain(self):
        for turn in range(4):
            for copy in self.copies(turn):
                copy.wait_send()


TABLES = {
    "pick": (128, 1024),
    "border": (128, 1024),
    "put_in": (1024, 128),
    "put": (1024, 256),
    "ring": (384, 128),
    "ring_back": (128, 768),
}
IMAGE = (32, 64, 128)
SHIFTED = (2, 36, 32, 384)
BUFFERS = {
    "source": (IMAGE, BF16),
    "upstream": (IMAGE, BF16),
    "first": ((3, 3, 128, 128), BF16),
    "second": ((3, 3, 128, 128), BF16),
    "first_fwd": ((4, 384, 256), BF16),
    "first_back": ((4, 384, 256), BF16),
    "second_fwd": ((4, 384, 256), BF16),
    "second_back": ((4, 384, 256), BF16),
    "shift_one": (SHIFTED, BF16),
    "shift_two": (SHIFTED, BF16),
    "shift_grad": (SHIFTED, BF16),
    "row_grad": ((2, 34, 32, 384), BF16),
    "turned_one": ((384, 2048), BF16),
    "turned_two": ((384, 2048), BF16),
    "hidden": (IMAGE, F32),
    "share": ((16, 64, 256), F32),
    "slope": (IMAGE, F32),
    "act": (IMAGE, BF16),
    "response": (IMAGE, BF16),
    "grad": (IMAGE, BF16),
    "field_grad": (IMAGE, BF16),
    "ring_one": ((4, 64, 384), BF16),
    "ring_two": ((4, 64, 384), BF16),
    "border_grad": ((4, 64, 128), BF16),
    "block": ((384, 384), F32),
    "leaving": ((4, 4, 32, 256), BF16),
    "arrived": ((4, 4, 32, 256), BF16),
}


class Names:
    def __init__(self, names, refs):
        for name, ref in zip(names, refs):
            setattr(self, name, ref)


def step_scratch():
    dma = pltpu.SemaphoreType.DMA
    return (
        [pltpu.VMEM(shape, BF16) for shape in TABLES.values()]
        + [pltpu.VMEM(shape, kind) for shape, kind in BUFFERS.values()]
        + [dma((4, 4)), dma((4, 4)), dma((6,))]
        + sum_scratch()
        + sum_scratch()
    )


def gelu_parts(hidden):
    bell = 0.5 * (1.0 + lax.erf(hidden * ROOT_HALF))
    return hidden * bell, bell + hidden * jnp.exp(-0.5 * hidden * hidden) * INV_ROOT_TAU


def each_pair(body, start=0):
    def step(pair, carry):
        for frame in range(2):
            carry = body(frame, pair, frame * 16 + pair, slice(frame * 128, (frame + 1) * 128), carry)
        return carry

    return lax.fori_loop(0, 16, step, start)


def fold_rows(value):
    return jnp.sum(value.reshape(8, 8, 128), axis=0)


def step_kernel(scale, edge_map, fields, cotangent, w_first, b_first, w_second, b_second,
                response_out, field_grad_out, kernel_one_out, bias_one_out, kernel_two_out,
                bias_two_out, *scratch):
    tables, scratch = Names(TABLES, scratch), scratch[len(TABLES) :]
    v, scratch = Names(BUFFERS, scratch), scratch[len(BUFFERS) :]
    halo = Halo(v.leaving, v.arrived, scratch[0], scratch[1])
    local_sem, scratch = scratch[2], scratch[3:]
    count = len(sum_scratch())
    sum_one, sum_two = GradientSum(scratch[:count]), GradientSum(scratch[count:])

    loads = [
        pltpu.make_async_copy(source, target, local_sem.at[index])
        for index, (source, target) in enumerate(
            ((fields, v.source), (w_first, v.first), (w_second, v.second), (cotangent, v.upstream))
        )
    ]
    for load in loads:
        load.start()
    mate, plane, column = sum_partners()
    partners = [*halo_partners(), mate, *plane, *column]
    barrier = pltpu.get_barrier_semaphore()
    for device in partners:
        pl.semaphore_signal(
            barrier, inc=1, device_id=device, device_id_type=pl.DeviceIdType.MESH
        )
    make_tables(edge_map, tables)
    loads[0].wait()
    v.leaving[0] = picked(tables.pick, v.source).reshape(4, 32, 256)
    pl.semaphore_wait(barrier, len(partners))
    halo.start(0)

    for shifted in (v.shift_one, v.shift_two, v.shift_grad):
        clear_rims(shifted)
    for frame in range(2):
        v.row_grad[frame, 32:34, :, 0:128] = jnp.zeros((2, 32, 128), BF16)
        v.row_grad[frame, 0:2, :, 256:384] = jnp.zeros((2, 32, 128), BF16)

    def shift_source(frame, pair, index, lanes, carry):
        lay_shifted(v.shift_one, frame, pair, v.source[index].astype(F32))
        return carry

    each_pair(shift_source)
    loads[1].wait()
    lay_weights(v.first_fwd, lambda row, col: v.first[row, col])
    tile_conv(v.shift_one, v.first_fwd, v.hidden)
    loads[2].wait()
    lay_weights(v.second_fwd, lambda row, col: v.second[row, col])
    halo.wait(0)
    halo_share(tables, v.arrived.at[0], v.first, v.ring_one, v.share)

    def activate(frame, pair, index, lanes, carry):
        hidden = v.hidden[index] + v.share[pair, :, lanes] + b_first[...]
        value, slope = gelu_parts(hidden)
        v.slope[index] = slope
        v.act[index] = value.astype(BF16)
        lay_shifted(v.shift_two, frame, pair, value)
        return carry

    each_pair(activate)
    v.leaving[1] = picked(tables.pick, v.act).reshape(4, 32, 256)
    halo.start(1)
    tile_conv(v.shift_two, v.second_fwd, v.hidden)
    lay_weights(v.second_back, lambda row, col: v.second[2 - row, 2 - col].T)
    lay_weights(v.first_back, lambda row, col: v.first[2 - row, 2 - col].T)
    loads[3].wait()
    halo.wait(1)
    halo_share(tables, v.arrived.at[1], v.second, v.ring_two, v.share)

    def respond(frame, pair, index, lanes, carry):
        hidden = v.hidden[index] + v.share[pair, :, lanes] + b_second[...]
        value, slope = gelu_parts(hidden)
        v.response[index] = value.astype(BF16)
        grad = (v.upstream[index].astype(F32) * slope).astype(BF16)
        v.grad[index] = grad
        wide = grad.astype(F32)
        lay_shifted(v.shift_grad, frame, pair, wide)
        lay_rows(v.row_grad, frame, pair, grad)
        return carry + fold_rows(wide)

    bias = each_pair(respond, jnp.zeros((8, 128), F32))
    bias = jnp.sum(bias, axis=0, keepdims=True)
    response_store = pltpu.make_async_copy(v.response, response_out, local_sem.at[4])
    response_store.start()
    ring_gradient(tables, v.grad, v.second, v.border_grad, v.leaving.at[2])
    halo.start(2)
    transpose_shifted(v.shift_two, v.turned_two)
    kernel_gradient(
        v.turned_two, v.row_grad, v.ring_two, v.border_grad, bias, v.block, sum_two.own
    )
    sum_two.start()
    tile_conv(v.shift_grad, v.second_back, v.hidden)
    transpose_shifted(v.shift_one, v.turned_one)
    sum_two.spread_plane()
    halo.wait(2)
    v.share[...] = dot(tables.put_in[...], v.arrived[2].reshape(128, 256)).reshape(16, 64, 256)

    def descend(frame, pair, index, lanes, carry):
        grad = ((v.hidden[index] + v.share[pair, :, lanes]) * v.slope[index]).astype(BF16)
        v.grad[index] = grad
        wide = grad.astype(F32)
        lay_shifted(v.shift_grad, frame, pair, wide)
        lay_rows(v.row_grad, frame, pair, grad)
        return carry + fold_rows(wide)

    bias = each_pair(descend, jnp.zeros((8, 128), F32))
    bias = jnp.sum(bias, axis=0, keepdims=True)
    ring_gradient(tables, v.grad, v.first, v.border_grad, v.leaving.at[3])
    halo.start(3)
    kernel_gradient(
        v.turned_one, v.row_grad, v.ring_one, v.border_grad, bias, v.block, sum_one.own
    )
    sum_one.start()
    sum_two.spread_column()
    sum_one.spread_plane()
    tile_conv(v.shift_grad, v.first_back, v.hidden)
    sum_two.gather_plane()
    sum_one.spread_column()
    halo.wait(3)
    v.share[...] = dot(tables.put_in[...], v.arrived[3].reshape(128, 256)).reshape(16, 64, 256)

    def finish(frame, pair, index, lanes, carry):
        v.field_grad[index] = (v.hidden[index] + v.share[pair, :, lanes]).astype(BF16)
        return carry

    each_pair(finish)
    field_grad_store = pltpu.make_async_copy(v.field_grad, field_grad_out, local_sem.at[5])
    field_grad_store.start()
    sum_two.forward()
    sum_one.gather_plane()
    sum_one.forward()
    for one, kernel_out, bias_out in (
        (sum_two, kernel_two_out, bias_two_out),
        (sum_one, kernel_one_out, bias_one_out),
    ):
        one.finish()
        full = one.gathered[...].reshape(PART_ROWS, 128)
        rows = kernel_out.shape[0]
        kernel_out[...] = full[:rows].astype(F32) * scale
        bias_out[...] = full[rows : rows + 8].astype(F32)[0:1] * scale
    response_store.wait()
    field_grad_store.wait()
    halo.drain()
    sum_one.drain()
    sum_two.drain()


def per_device(fields, cotangent, edge_map, w_first, b_first, w_second, b_second):
    frames, tile_side, channels = (fields.shape[2], fields.shape[3], fields.shape[5])
    samples = lax.axis_size("tile") * lax.axis_size("member") * frames * tile_side * tile_side
    kernel = jax.ShapeDtypeStruct((9 * channels, channels), F32)
    bias = jax.ShapeDtypeStruct((1, channels), F32)
    image = jax.ShapeDtypeStruct(IMAGE, BF16)
    anywhere = pl.BlockSpec(memory_space=pl.ANY)
    local = pl.BlockSpec(memory_space=pltpu.VMEM)
    outs = pl.pallas_call(
        functools.partial(step_kernel, float(samples) ** -0.5),
        out_shape=[image, image, kernel, bias, kernel, bias],
        in_specs=[
            pl.BlockSpec(memory_space=pltpu.SMEM),
            anywhere,
            anywhere,
            anywhere,
            local,
            anywhere,
            local,
        ],
        out_specs=[anywhere, anywhere, local, local, local, local],
        scratch_shapes=step_scratch(),
        compiler_params=pltpu.CompilerParams(collective_id=0, has_side_effects=True),
    )(
        edge_map.reshape(4, 2),
        fields.reshape(IMAGE),
        cotangent.reshape(IMAGE),
        w_first,
        b_first.reshape(1, channels),
        w_second,
        b_second.reshape(1, channels),
    )
    return (
        outs[0].reshape(fields.shape),
        outs[1].reshape(fields.shape),
        outs[2].reshape(w_first.shape),
        outs[3].reshape(b_first.shape),
        outs[4].reshape(w_second.shape),
        outs[5].reshape(b_second.shape),
    )


def solution(mesh):
    in_specs = (
        P("member", "tile", None, None, None, None),
        P("member", "tile", None, None, None, None),
        P("tile", None, None),
        P(),
        P(),
        P(),
        P(),
    )
    out_specs = (
        P("member", "tile", None, None, None, None),
        P("member", "tile", None, None, None, None),
        P(),
        P(),
        P(),
        P(),
    )
    return jax.shard_map(
        per_device, mesh=mesh, in_specs=in_specs, out_specs=out_specs, check_vma=False
    )
```

profile of v0, /device:TPU:1, one launch (start us, length us, event | category | flops | bytes accessed | tf_op | source)
XLA Modules:
  0.0 65.2 jit_solution(14550863809362234893)
XLA Ops:
  0.6 0.0 copy-start.3
  0.6 0.7 %copy-done.3 = s32[1,4,2]{1,2,0:T(2,128)S(1)} copy-done((s32[1,4,2]{1,2,0:T(2,128)S(1)}, s32[1,4,2]{1,2,0:T(2,128)}, u32[]{:S(2)}) %copy-start.3) | copy-done | bytes 56
  1.3 0.7 %copy.13.edge_map = s32[4,2]{1,0:T(4,128)} copy(s32[4,2]{0,1:T(2,128)S(1)} %bitcast.17) | data formatting | bytes 64 | tf_op jit(solution)/shard_map/reshape | solution.py:695
  2.0 57.4 %shard_map.118 = (bf16[32,64,128]{2,1,0:T(8,128)(2,1)}, bf16[32,64,128]{2,1,0:T(8,128)(2,1)}, f32[1152,128]{1,0:T(8,128)}, f32[1,128]{1,0:T(1,128)}, f32[1152,128]{1,0:T(8,128)}, /*index=5*/f32[1,128]{1,0:T(1,128)}) custom-call(s32[4,2]{1,0:T(4,128)} %copy.13.edge_map, bf16[32,64,128]{2,1,0:T(8,128)(2,1)} %bitcast.13, bf16[32,64,128]{2,1,0:T(8,128)(2,1)} %bitcast.14, ...), custom_call_target="tpu_custom_call" | custom-call | tf_op jit(solution)/shard_map/pallas_call | solution.py:679
  59.4 0.0 copy-start.2
  59.4 1.9 %copy.20 = bf16[1,1,2,32,32,128]{5,4,3,2,1,0:T(8,128)(2,1)} copy(bf16[1,1,2,32,32,128]{5,4,3,2,1,0:T(8,128)(2,1)} %bitcast.16) | data formatting | bytes 1048576
  61.3 0.0 copy-done.2
  61.3 0.0 copy-start.1
  61.3 0.8 %copy.21 = bf16[1,1,2,32,32,128]{5,4,3,2,1,0:T(8,128)(2,1)} copy(bf16[1,1,2,32,32,128]{5,4,3,2,1,0:T(8,128)(2,1)S(1)} %bitcast.15) | data formatting | bytes 1048576
  62.1 0.5 copy-done.1
  62.6 0.0 copy-start.5
  62.6 0.0 copy-start
  62.6 0.8 %copy.22 = f32[3,3,128,128]{3,2,1,0:T(8,128)} copy(f32[3,3,128,128]{3,2,1,0:T(8,128)S(1)} %bitcast.12) | data formatting | bytes 1179648
  63.4 0.0 copy-done.5
  63.4 0.5 copy.23
  63.9 0.0 copy-done
  63.9 0.0 copy-start.4
  63.9 0.8 %copy.24 = f32[3,3,128,128]{3,2,1,0:T(8,128)} copy(f32[3,3,128,128]{3,2,1,0:T(8,128)S(1)} %bitcast.11) | data formatting | bytes 1179648
  64.7 0.0 copy-done.4
  64.7 0.5 copy.25
Async XLA Ops:
  0.6 0.7 %copy-start.3 = (s32[1,4,2]{1,2,0:T(2,128)S(1)}, s32[1,4,2]{1,2,0:T(2,128)}, u32[]{:S(2)}) copy-start(s32[1,4,2]{1,2,0:T(2,128)} %param.9) | copy-start | bytes 100
  59.4 1.9 %copy-start.2 = (bf16[32,64,128]{2,1,0:T(8,128)(2,1)S(1)}, bf16[32,64,128]{2,1,0:T(8,128)(2,1)}, u32[]{:S(2)}) copy-start(bf16[32,64,128]{2,1,0:T(8,128)(2,1)} %get-tuple-element.13) | copy-start | bytes 1572868
  61.3 1.3 %copy-start.1 = (f32[1152,128]{1,0:T(8,128)S(1)}, f32[1152,128]{1,0:T(8,128)}, u32[]{:S(2)}) copy-start(f32[1152,128]{1,0:T(8,128)} %get-tuple-element.14) | copy-start | bytes 1769476
  62.6 0.8 %copy-start.5 = (f32[1,128]{1,0:T(1,128)S(1)}, f32[1,128]{1,0:T(1,128)}, u32[]{:S(2)}) copy-start(f32[1,128]{1,0:T(1,128)} %get-tuple-element.15) | copy-start | bytes 1540
  62.6 1.3 %copy-start = (f32[1152,128]{1,0:T(8,128)S(1)}, f32[1152,128]{1,0:T(8,128)}, u32[]{:S(2)}) copy-start(f32[1152,128]{1,0:T(8,128)} %get-tuple-element.16) | copy-start | bytes 1769476
  63.9 0.8 %copy-start.4 = (f32[1,128]{1,0:T(1,128)S(1)}, f32[1,128]{1,0:T(1,128)}, u32[]{:S(2)}) copy-start(f32[1,128]{1,0:T(1,128)} %get-tuple-element.17) | copy-start | bytes 1540
where the time goes:
time: 65.4 us; the launch traced here: 65.2 us
  Pallas kernels  57.4 us (88%)
  local copies, waits for them, and re-layouts  7.18 us (11%)
  between operations  0.66 us (1%)
    pallas_call x1, Pallas kernels, per_device(): pl.pallas_call(functools.partial(step_kernel, float(samples) ** (-0.5)),...  57.4 us
    unnamed x18, local copies, waits for them, and re-layouts  6.52 us

commit v1 on v0

--- a/solution.py
+++ b/solution.py
@@ -229,8 +229,8 @@
     side = jnp.zeros_like(index)
     flip = jnp.zeros_like(index)
     for candidate in range(4):
-        side = jnp.where(direction == candidate, edge_map[candidate, 0], side)
-        flip = jnp.where(direction == candidate, edge_map[candidate, 1], flip)
+        side = jnp.where(direction == candidate, edge_map[0, candidate], side)
+        flip = jnp.where(direction == candidate, edge_map[1, candidate], flip)
     return side, jnp.where(flip == 1, 31 - place, place)
 
 
@@ -475,9 +475,7 @@
     "share": ((16, 64, 256), F32),
     "slope": (IMAGE, F32),
     "act": (IMAGE, BF16),
-    "response": (IMAGE, BF16),
     "grad": (IMAGE, BF16),
-    "field_grad": (IMAGE, BF16),
     "ring_one": ((4, 64, 384), BF16),
     "ring_two": ((4, 64, 384), BF16),
     "border_grad": ((4, 64, 128), BF16),
@@ -498,7 +496,7 @@
     return (
         [pltpu.VMEM(shape, BF16) for shape in TABLES.values()]
         + [pltpu.VMEM(shape, kind) for shape, kind in BUFFERS.values()]
-        + [dma((4, 4)), dma((4, 4)), dma((6,))]
+        + [dma((4, 4)), dma((4, 4)), dma((4,))]
         + sum_scratch()
         + sum_scratch()
     )
@@ -522,9 +520,8 @@
     return jnp.sum(value.reshape(8, 8, 128), axis=0)
 
 
-def step_kernel(scale, edge_map, fields, cotangent, w_first, b_first, w_second, b_second,
-                response_out, field_grad_out, kernel_one_out, bias_one_out, kernel_two_out,
-                bias_two_out, *scratch):
+def step_kernel(edge_map, fields, cotangent, w_first, b_first, w_second, b_second,
+                response_out, field_grad_out, sum_one_out, sum_two_out, *scratch):
     tables, scratch = Names(TABLES, scratch), scratch[len(TABLES) :]
     v, scratch = Names(BUFFERS, scratch), scratch[len(BUFFERS) :]
     halo = Halo(v.leaving, v.arrived, scratch[0], scratch[1])
@@ -593,7 +590,7 @@
     def respond(frame, pair, index, lanes, carry):
         hidden = v.hidden[index] + v.share[pair, :, lanes] + b_second[...]
         value, slope = gelu_parts(hidden)
-        v.response[index] = value.astype(BF16)
+        response_out[index] = value.astype(BF16)
         grad = (v.upstream[index].astype(F32) * slope).astype(BF16)
         v.grad[index] = grad
         wide = grad.astype(F32)
@@ -603,8 +600,6 @@
 
     bias = each_pair(respond, jnp.zeros((8, 128), F32))
     bias = jnp.sum(bias, axis=0, keepdims=True)
-    response_store = pltpu.make_async_copy(v.response, response_out, local_sem.at[4])
-    response_store.start()
     ring_gradient(tables, v.grad, v.second, v.border_grad, v.leaving.at[2])
     halo.start(2)
     transpose_shifted(v.shift_two, v.turned_two)
@@ -643,56 +638,72 @@
     v.share[...] = dot(tables.put_in[...], v.arrived[3].reshape(128, 256)).reshape(16, 64, 256)
 
     def finish(frame, pair, index, lanes, carry):
-        v.field_grad[index] = (v.hidden[index] + v.share[pair, :, lanes]).astype(BF16)
+        field_grad_out[index] = (v.hidden[index] + v.share[pair, :, lanes]).astype(BF16)
         return carry
 
     each_pair(finish)
-    field_grad_store = pltpu.make_async_copy(v.field_grad, field_grad_out, local_sem.at[5])
-    field_grad_store.start()
     sum_two.forward()
     sum_one.gather_plane()
     sum_one.forward()
-    for one, kernel_out, bias_out in (
-        (sum_two, kernel_two_out, bias_two_out),
-        (sum_one, kernel_one_out, bias_one_out),
-    ):
+    for one, out in ((sum_two, sum_two_out), (sum_one, sum_one_out)):
         one.finish()
-        full = one.gathered[...].reshape(PART_ROWS, 128)
-        rows = kernel_out.shape[0]
-        kernel_out[...] = full[:rows].astype(F32) * scale
-        bias_out[...] = full[rows : rows + 8].astype(F32)[0:1] * scale
-    response_store.wait()
-    field_grad_store.wait()
+        out[...] = one.gathered[...].reshape(2 * HALF, 8, 128)
     halo.drain()
     sum_one.drain()
     sum_two.drain()
 
 
+def store_kernel(scale, response, field_grad, sum_one, sum_two, response_out, field_grad_out,
+                 kernel_one_out, bias_one_out, kernel_two_out, bias_two_out, kernel_one,
+                 bias_one, kernel_two, bias_two, sems):
+    stores = [
+        pltpu.make_async_copy(response, response_out, sems.at[0]),
+        pltpu.make_async_copy(field_grad, field_grad_out, sems.at[1]),
+    ]
+    for store in stores:
+        store.start()
+    for total, kernel, bias, kernel_out, bias_out in (
+        (sum_one, kernel_one, bias_one, kernel_one_out, bias_one_out),
+        (sum_two, kernel_two, bias_two, kernel_two_out, bias_two_out),
+    ):
+        kernel[...] = total[0:144].astype(F32) * scale
+        bias[...] = total[144].astype(F32)[0:1] * scale
+        for source, target in ((kernel, kernel_out), (bias, bias_out)):
+            stores.append(pltpu.make_async_copy(source, target, sems.at[len(stores)]))
+            stores[-1].start()
+    for store in stores:
+        store.wait()
+
+
 def per_device(fields, cotangent, edge_map, w_first, b_first, w_second, b_second):
     frames, tile_side, channels = (fields.shape[2], fields.shape[3], fields.shape[5])
     samples = lax.axis_size("tile") * lax.axis_size("member") * frames * tile_side * tile_side
-    kernel = jax.ShapeDtypeStruct((9 * channels, channels), F32)
+    kernel = jax.ShapeDtypeStruct((9 * channels // 8, 8, channels), F32)
     bias = jax.ShapeDtypeStruct((1, channels), F32)
     image = jax.ShapeDtypeStruct(IMAGE, BF16)
-    anywhere = pl.BlockSpec(memory_space=pl.ANY)
     local = pl.BlockSpec(memory_space=pltpu.VMEM)
-    outs = pl.pallas_call(
-        functools.partial(step_kernel, float(samples) ** -0.5),
-        out_shape=[image, image, kernel, bias, kernel, bias],
+    far = pl.BlockSpec(memory_space=pltpu.HBM)
+    near = pltpu.VMEM(IMAGE, BF16)
+    sums = pltpu.VMEM((2 * HALF, 8, 128), BF16)
+    results = pl.pallas_call(
+        step_kernel,
+        out_shape=[near, near, sums, sums],
         in_specs=[
             pl.BlockSpec(memory_space=pltpu.SMEM),
-            anywhere,
-            anywhere,
-            anywhere,
+            far,
+            far,
+            far,
             local,
-            anywhere,
+            far,
             local,
         ],
-        out_specs=[anywhere, anywhere, local, local, local, local],
+        out_specs=[local] * 4,
         scratch_shapes=step_scratch(),
-        compiler_params=pltpu.CompilerParams(collective_id=0, has_side_effects=True),
+        compiler_params=pltpu.CompilerParams(
+            collective_id=0, has_side_effects=True, vmem_limit_bytes=63_600 << 10
+        ),
     )(
-        edge_map.reshape(4, 2),
+        edge_map.reshape(4, 2).T,
         fields.reshape(IMAGE),
         cotangent.reshape(IMAGE),
         w_first,
@@ -700,6 +711,20 @@
         w_second,
         b_second.reshape(1, channels),
     )
+    outs = pl.pallas_call(
+        functools.partial(store_kernel, float(samples) ** -0.5),
+        out_shape=[image, image, kernel, bias, kernel, bias],
+        in_specs=[local] * 4,
+        out_specs=[far] * 6,
+        scratch_shapes=[
+            pltpu.VMEM(kernel.shape, F32),
+            pltpu.VMEM(bias.shape, F32),
+            pltpu.VMEM(kernel.shape, F32),
+            pltpu.VMEM(bias.shape, F32),
+            pltpu.SemaphoreType.DMA((6,)),
+        ],
+        compiler_params=pltpu.CompilerParams(vmem_limit_bytes=8 << 20),
+    )(*results)
     return (
         outs[0].reshape(fields.shape),
         outs[1].reshape(fields.shape),

time: 65.4 us -> 58.6 us (0.90)
  local copies, waits for them, and re-layouts: 7.18 us -> 0 us
    unnamed x18 -> x0, local copies, waits for them, and re-layouts: 6.52 us -> none
    reshape x1 -> x0, local copies, waits for them, and re-layouts: 0.66 us -> none  [per_device(): edge_map.reshape(4, 2)]
    pallas_call x1 -> x2, Pallas kernels: 57.4 us -> 57.9 us  [the longest x1 56.5 us: per_device(): pl.pallas_call(step_kernel, out_shape=[near, near, sums, sums], in_specs=...]
where the time goes in v1:
time: 58.6 us; the launch traced here: 58.5 us
  Pallas kernels  57.9 us (99%)
  between operations  0.64 us (1%)
    pallas_call x1, Pallas kernels, per_device(): pl.pallas_call(step_kernel, out_shape=[near, near, sums, sums], in_specs=...  56.5 us
    pallas_call x1, Pallas kernels, per_device(): pl.pallas_call(functools.partial(store_kernel, float(samples) ** (-0.5)),...  1.42 us

profile of v1, /device:TPU:1, one launch (start us, length us, event | category | flops | bytes accessed | tf_op | source)
XLA Modules:
  0.0 58.5 jit_solution(5264553089548989181)
XLA Ops:
  0.6 56.5 %shard_map.118 = (bf16[32,64,128]{2,1,0:T(8,128)(2,1)S(1)}, bf16[32,64,128]{2,1,0:T(8,128)(2,1)S(1)}, bf16[160,8,128]{2,1,0:T(8,128)(2,1)S(1)}, bf16[160,8,128]{2,1,0:T(8,128)(2,1)S(1)}) custom-call(s32[2,4]{1,0:T(2,128)} %bitcast.15, bf16[32,64,128]{2,1,0:T(8,128)(2,1)} %bitcast.13, bf16[32,64,128]{2,1,0:T(8,128)(2,1)} %bitcast.14, ...), custom_call_target="tpu_custom_call" | custom-call | tf_op jit(solution)/shard_map/pallas_call | solution.py:688
  57.1 1.4 %shard_map.119 = (bf16[32,64,128]{2,1,0:T(8,128)(2,1)}, bf16[32,64,128]{2,1,0:T(8,128)(2,1)}, f32[144,8,128]{2,1,0:T(8,128)}, f32[1,128]{1,0:T(1,128)}, f32[144,8,128]{2,1,0:T(8,128)}, /*index=5*/f32[1,128]{1,0:T(1,128)}) custom-call(bf16[32,64,128]{2,1,0:T(8,128)(2,1)S(1)} %get-tuple-element.16.response, ...), custom_call_target="tpu_custom_call" | custom-call | tf_op jit(solution)/shard_map/pallas_call | solution.py:714

commit v2 on v1

--- a/solution.py
+++ b/solution.py
@@ -67,10 +67,10 @@
         pltpu.VMEM((DEPTH, PIECE, 8, 128), jnp.bfloat16),
         pltpu.VMEM((2, PLANE, PIECE, 8, 128), jnp.bfloat16),
         dma((2,)),
-        dma((2, PLANE)),
-        dma((2, DEPTH)),
-        dma((2, PLANE)),
-        dma((2, PLANE)),
+        dma((2,)),
+        dma((2,)),
+        dma((2,)),
+        dma((2,)),
     ]
 
 
@@ -109,8 +109,8 @@
         return remote(
             self.pieces.at[target],
             self.from_plane.at[self.spot],
-            self.plane_sem.at[0, step],
-            self.plane_sem.at[1, step],
+            self.plane_sem.at[0],
+            self.plane_sem.at[1],
             self.plane[step - 1],
         )
 
@@ -118,8 +118,8 @@
         return remote(
             self.from_column.at[self.level],
             self.from_column.at[self.level],
-            self.column_sem.at[0, step],
-            self.column_sem.at[1, step],
+            self.column_sem.at[0],
+            self.column_sem.at[1],
             self.column[step - 1],
         )
 
@@ -127,20 +127,24 @@
         return remote(
             self.gathered.at[self.core, self.spot],
             self.gathered.at[self.core, self.spot],
-            self.gather_sem.at[0, step],
-            self.gather_sem.at[1, step],
+            self.gather_sem.at[0],
+            self.gather_sem.at[1],
             self.plane[step - 1],
         )
 
-    def to_forward(self, step):
-        origin = lax.rem(self.spot + PLANE - step, PLANE)
+    def to_forward(self):
         return remote(
-            self.gathered.at[self.core, origin],
-            self.gathered.at[self.core, origin],
-            self.forward_sem.at[0, step],
-            self.forward_sem.at[1, step],
+            self.gathered.at[self.core],
+            self.gathered.at[self.core],
+            self.forward_sem.at[0],
+            self.forward_sem.at[1],
             self.mate,
         )
+
+    def wait_all(self, buffer, count, sem):
+        pltpu.make_async_copy(
+            buffer.at[pl.ds(0, count)], buffer.at[pl.ds(0, count)], sem
+        ).wait()
 
     def start(self):
         self.halves[...] = self.own[...].astype(jnp.bfloat16)
@@ -157,8 +161,8 @@
 
     def spread_column(self):
         value = self.total[self.spot]
+        self.wait_all(self.from_plane, PLANE - 1, self.plane_sem.at[1])
         for step in range(1, PLANE):
-            self.to_plane(step).wait_recv()
             origin = lax.rem(self.spot + PLANE - step, PLANE)
             value = value + self.from_plane[origin].astype(jnp.float32)
         self.from_column[self.level] = value.astype(jnp.bfloat16)
@@ -166,34 +170,27 @@
             self.to_column(step).start()
 
     def gather_plane(self):
-        for step in range(1, DEPTH):
-            self.to_column(step).wait_recv()
+        self.wait_all(self.from_column, DEPTH - 1, self.column_sem.at[1])
         value = jnp.zeros((PIECE, 8, 128), jnp.float32)
         for level in range(DEPTH):
             value = value + self.from_column[level].astype(jnp.float32)
         self.gathered[self.core, self.spot] = value.astype(jnp.bfloat16)
         for step in range(1, PLANE):
             self.to_gather(step).start()
-        self.to_forward(0).start()
 
     def forward(self):
-        for step in range(1, PLANE):
-            self.to_gather(step).wait_recv()
-            self.to_forward(step).start()
+        self.wait_all(self.gathered.at[self.core], PLANE - 1, self.gather_sem.at[1])
+        self.to_forward().start()
 
     def finish(self):
-        for step in range(PLANE):
-            self.to_forward(step).wait_recv()
+        self.to_forward().wait_recv()
 
     def drain(self):
         self.to_mate().wait_send()
-        for step in range(1, PLANE):
-            self.to_plane(step).wait_send()
-            self.to_gather(step).wait_send()
-        for step in range(1, DEPTH):
-            self.to_column(step).wait_send()
-        for step in range(PLANE):
-            self.to_forward(step).wait_send()
+        self.wait_all(self.pieces, PLANE - 1, self.plane_sem.at[0])
+        self.wait_all(self.from_column, DEPTH - 1, self.column_sem.at[0])
+        self.wait_all(self.gathered.at[self.core], PLANE - 1, self.gather_sem.at[0])
+        self.to_forward().wait_send()
 
 
 def dot(left, right):
@@ -264,6 +261,7 @@
     pixel = border_pixel(side, place)
     plain = border_pixel(row >> 5, row & 31)
     turn = ones_where(lane == side * 32 + place)
+    t.turn[...] = turn
     for block in range(8):
         here = lane + block * 128
         t.pick[:, block * 128 : (block + 1) * 128] = ones_where(here == pixel)
@@ -278,6 +276,10 @@
         marks = ones_where(here == lane_plain)
         t.put[rows, 0:128] = marks
         t.put[rows, 128:256] = marks
+    cross = dot_nt(t.border[...], t.border[...]).astype(BF16)
+    t.cross[:, 0:128] = cross
+    t.cross[:, 128:256] = cross
+    t.cross_in[...] = dot_nt(t.border[...], t.pick[...]).astype(BF16)
     for tap in range(3):
         taps = ring_taps(tap)
         t.ring[tap * 128 : (tap + 1) * 128, :] = dot_nt(taps, turn).astype(BF16)
@@ -327,9 +329,11 @@
             rows = shifted[frame, row : row + 32].reshape(16, 2, 32, 384)[:, 0].reshape(512, 384)
             part = dot(rows, weights[row])
             total = part if total is None else total + part
-        pairs = slice(frame * 16, (frame + 1) * 16)
-        result[pairs, 0:32, :] = total[:, 0:128].reshape(16, 32, 128)
-        result[pairs, 32:64, :] = total[:, 128:256].reshape(16, 32, 128)
+        for pair in range(16):
+            first = frame * 1024 + pair * 64
+            rows = slice(pair * 32, (pair + 1) * 32)
+            result[first : first + 32, :] = total[rows, 0:128]
+            result[first + 32 : first + 64, :] = total[rows, 128:256]
 
 
 def transpose_shifted(shifted, target):
@@ -349,7 +353,7 @@
     return jnp.concatenate(parts, axis=1).astype(BF16)
 
 
-def halo_share(t, arrived, weights, ring_rows, share):
+def halo_share(t, arrived, weights, ring_rows):
     around = dot(t.ring[...], arrived[...].reshape(128, 256)).astype(BF16)
     parts = []
     for side in range(4):
@@ -365,16 +369,18 @@
         taps = jnp.concatenate([weights[side_tap(side, tap)] for tap in range(3)], axis=0)
         value = dot(ring_rows[side], taps)
         parts.append(jnp.concatenate([value[0:32], value[32:64]], axis=1))
-    both = split_float(jnp.concatenate(parts, axis=0))
-    share[...] = dot(t.put[...], both).reshape(16, 64, 256)
-
-
-def ring_gradient(t, image, weights, border_rows, leaving):
-    border = picked(t.border, image)
-    rows = [[None] * 4 for tap in range(3)]
+    return split_float(jnp.concatenate(parts, axis=0))
+
+
+def lay_border(border, border_rows):
     for side in range(4):
         here = border[side * 32 : (side + 1) * 32]
         border_rows[side] = jnp.concatenate([here[:, 0:128], here[:, 128:256]], axis=0)
+
+
+def ring_gradient(t, weights, border_rows, leaving):
+    rows = [[None] * 4 for tap in range(3)]
+    for side in range(4):
         for tap in range(3):
             value = dot_nt(border_rows[side], weights[side_tap(side, tap)])
             rows[tap][side] = jnp.concatenate([value[0:32], value[32:64]], axis=1)
@@ -451,6 +457,9 @@
     "border": (128, 1024),
     "put_in": (1024, 128),
     "put": (1024, 256),
+    "turn": (128, 128),
+    "cross": (128, 256),
+    "cross_in": (128, 128),
     "ring": (384, 128),
     "ring_back": (128, 768),
 }
@@ -471,11 +480,14 @@
     "row_grad": ((2, 34, 32, 384), BF16),
     "turned_one": ((384, 2048), BF16),
     "turned_two": ((384, 2048), BF16),
-    "hidden": (IMAGE, F32),
+    "hidden": ((2048, 128), F32),
+    "hidden_border": ((128, 256), F32),
+    "slope_border": ((128, 256), F32),
+    "upstream_border": ((128, 256), BF16),
+    "both": ((256, 256), BF16),
+    "grad": (IMAGE, BF16),
     "share": ((16, 64, 256), F32),
     "slope": (IMAGE, F32),
-    "act": (IMAGE, BF16),
-    "grad": (IMAGE, BF16),
     "ring_one": ((4, 64, 384), BF16),
     "ring_two": ((4, 64, 384), BF16),
     "border_grad": ((4, 64, 128), BF16),
@@ -507,6 +519,32 @@
     return hidden * bell, bell + hidden * jnp.exp(-0.5 * hidden * hidden) * INV_ROOT_TAU
 
 
+def rows_of(index):
+    return pl.ds(pl.multiple_of(index * 64, 64), 64)
+
+
+def twice(bias):
+    return jnp.concatenate([bias, bias], axis=1)
+
+
+def border_of(image):
+    frames = []
+    for frame in range(2):
+        first = frame * 1024
+        frames.append(
+            jnp.concatenate(
+                [
+                    image[first : first + 32, :],
+                    image[pl.ds(first + 31, 32, stride=32), :],
+                    image[first + 992 : first + 1024, :],
+                    image[pl.ds(first, 32, stride=32), :],
+                ],
+                axis=0,
+            )
+        )
+    return jnp.concatenate(frames, axis=1)
+
+
 def each_pair(body, start=0):
     def step(pair, carry):
         for frame in range(2):
@@ -529,6 +567,13 @@
     count = len(sum_scratch())
     sum_one, sum_two = GradientSum(scratch[:count]), GradientSum(scratch[count:])
 
+    mate, plane, column = sum_partners()
+    partners = [*halo_partners(), mate, *plane, *column]
+    barrier = pltpu.get_barrier_semaphore()
+    for device in partners:
+        pl.semaphore_signal(
+            barrier, inc=1, device_id=device, device_id_type=pl.DeviceIdType.MESH
+        )
     loads = [
         pltpu.make_async_copy(source, target, local_sem.at[index])
         for index, (source, target) in enumerate(
@@ -537,13 +582,6 @@
     ]
     for load in loads:
         load.start()
-    mate, plane, column = sum_partners()
-    partners = [*halo_partners(), mate, *plane, *column]
-    barrier = pltpu.get_barrier_semaphore()
-    for device in partners:
-        pl.semaphore_signal(
-            barrier, inc=1, device_id=device, device_id_type=pl.DeviceIdType.MESH
-        )
     make_tables(edge_map, tables)
     loads[0].wait()
     v.leaving[0] = picked(tables.pick, v.source).reshape(4, 32, 256)
@@ -564,35 +602,51 @@
     loads[1].wait()
     lay_weights(v.first_fwd, lambda row, col: v.first[row, col])
     tile_conv(v.shift_one, v.first_fwd, v.hidden)
+    v.hidden_border[...] = border_of(v.hidden) + twice(b_first[...])
     loads[2].wait()
     lay_weights(v.second_fwd, lambda row, col: v.second[row, col])
+    loads[3].wait()
+    v.upstream_border[...] = picked(tables.border, v.upstream)
+    transpose_shifted(v.shift_one, v.turned_one)
+    lay_weights(v.second_back, lambda row, col: v.second[2 - row, 2 - col].T)
+    lay_weights(v.first_back, lambda row, col: v.first[2 - row, 2 - col].T)
+
     halo.wait(0)
-    halo_share(tables, v.arrived.at[0], v.first, v.ring_one, v.share)
+    both = halo_share(tables, v.arrived.at[0], v.first, v.ring_one)
+    v.both[...] = both
+    value, slope = gelu_parts(v.hidden_border[...] + dot(tables.cross[...], both))
+    v.leaving[1] = dot(tables.turn[...], value.astype(BF16)).astype(BF16).reshape(4, 32, 256)
+    v.slope_border[...] = slope
+    halo.start(1)
+    v.share[...] = dot(tables.put[...], v.both[...]).reshape(16, 64, 256)
 
     def activate(frame, pair, index, lanes, carry):
-        hidden = v.hidden[index] + v.share[pair, :, lanes] + b_first[...]
+        hidden = v.hidden[rows_of(index)] + v.share[pair, :, lanes] + b_first[...]
         value, slope = gelu_parts(hidden)
         v.slope[index] = slope
-        v.act[index] = value.astype(BF16)
         lay_shifted(v.shift_two, frame, pair, value)
         return carry
 
     each_pair(activate)
-    v.leaving[1] = picked(tables.pick, v.act).reshape(4, 32, 256)
-    halo.start(1)
     tile_conv(v.shift_two, v.second_fwd, v.hidden)
-    lay_weights(v.second_back, lambda row, col: v.second[2 - row, 2 - col].T)
-    lay_weights(v.first_back, lambda row, col: v.first[2 - row, 2 - col].T)
-    loads[3].wait()
+    v.hidden_border[...] = border_of(v.hidden) + twice(b_second[...])
+    transpose_shifted(v.shift_two, v.turned_two)
+
     halo.wait(1)
-    halo_share(tables, v.arrived.at[1], v.second, v.ring_two, v.share)
+    both = halo_share(tables, v.arrived.at[1], v.second, v.ring_two)
+    v.both[...] = both
+    value, slope = gelu_parts(v.hidden_border[...] + dot(tables.cross[...], both))
+    border = (v.upstream_border[...].astype(F32) * slope).astype(BF16)
+    lay_border(border, v.border_grad)
+    ring_gradient(tables, v.second, v.border_grad, v.leaving.at[2])
+    halo.start(2)
+    v.share[...] = dot(tables.put[...], v.both[...]).reshape(16, 64, 256)
 
     def respond(frame, pair, index, lanes, carry):
-        hidden = v.hidden[index] + v.share[pair, :, lanes] + b_second[...]
+        hidden = v.hidden[rows_of(index)] + v.share[pair, :, lanes] + b_second[...]
         value, slope = gelu_parts(hidden)
         response_out[index] = value.astype(BF16)
         grad = (v.upstream[index].astype(F32) * slope).astype(BF16)
-        v.grad[index] = grad
         wide = grad.astype(F32)
         lay_shifted(v.shift_grad, frame, pair, wide)
         lay_rows(v.row_grad, frame, pair, grad)
@@ -600,57 +654,66 @@
 
     bias = each_pair(respond, jnp.zeros((8, 128), F32))
     bias = jnp.sum(bias, axis=0, keepdims=True)
-    ring_gradient(tables, v.grad, v.second, v.border_grad, v.leaving.at[2])
-    halo.start(2)
-    transpose_shifted(v.shift_two, v.turned_two)
+    tile_conv(v.shift_grad, v.second_back, v.hidden)
+    v.hidden_border[...] = border_of(v.hidden)
     kernel_gradient(
         v.turned_two, v.row_grad, v.ring_two, v.border_grad, bias, v.block, sum_two.own
     )
     sum_two.start()
-    tile_conv(v.shift_grad, v.second_back, v.hidden)
-    transpose_shifted(v.shift_one, v.turned_one)
+
     sum_two.spread_plane()
+
     halo.wait(2)
-    v.share[...] = dot(tables.put_in[...], v.arrived[2].reshape(128, 256)).reshape(16, 64, 256)
+    came = v.arrived[2].reshape(128, 256)
+    border = v.hidden_border[...] + dot(tables.cross_in[...], came)
+    border = (border * v.slope_border[...]).astype(BF16)
+    lay_border(border, v.border_grad)
+    v.share[...] = dot(tables.put_in[...], came).reshape(16, 64, 256)
 
     def descend(frame, pair, index, lanes, carry):
-        grad = ((v.hidden[index] + v.share[pair, :, lanes]) * v.slope[index]).astype(BF16)
+        grad = v.hidden[rows_of(index)] + v.share[pair, :, lanes]
+        grad = (grad * v.slope[index]).astype(BF16)
         v.grad[index] = grad
-        wide = grad.astype(F32)
-        lay_shifted(v.shift_grad, frame, pair, wide)
         lay_rows(v.row_grad, frame, pair, grad)
-        return carry + fold_rows(wide)
+        return carry + fold_rows(grad.astype(F32))
 
     bias = each_pair(descend, jnp.zeros((8, 128), F32))
     bias = jnp.sum(bias, axis=0, keepdims=True)
-    ring_gradient(tables, v.grad, v.first, v.border_grad, v.leaving.at[3])
-    halo.start(3)
     kernel_gradient(
         v.turned_one, v.row_grad, v.ring_one, v.border_grad, bias, v.block, sum_one.own
     )
     sum_one.start()
+    ring_gradient(tables, v.first, v.border_grad, v.leaving.at[3])
+    halo.start(3)
+
+    def shift_grad(frame, pair, index, lanes, carry):
+        lay_shifted(v.shift_grad, frame, pair, v.grad[index].astype(F32))
+        return carry
+
+    sum_one.spread_plane()
+    each_pair(shift_grad)
     sum_two.spread_column()
-    sum_one.spread_plane()
     tile_conv(v.shift_grad, v.first_back, v.hidden)
-    sum_two.gather_plane()
-    sum_one.spread_column()
     halo.wait(3)
     v.share[...] = dot(tables.put_in[...], v.arrived[3].reshape(128, 256)).reshape(16, 64, 256)
+    sum_one.spread_column()
 
     def finish(frame, pair, index, lanes, carry):
-        field_grad_out[index] = (v.hidden[index] + v.share[pair, :, lanes]).astype(BF16)
+        field_grad_out[index] = (v.hidden[rows_of(index)] + v.share[pair, :, lanes]).astype(BF16)
         return carry
 
     each_pair(finish)
+    sum_two.gather_plane()
+    sum_one.gather_plane()
+    halo.drain()
     sum_two.forward()
-    sum_one.gather_plane()
+    sum_two.finish()
+    sum_two_out[...] = sum_two.gathered[...].reshape(2 * HALF, 8, 128)
+    sum_two.drain()
     sum_one.forward()
-    for one, out in ((sum_two, sum_two_out), (sum_one, sum_one_out)):
-        one.finish()
-        out[...] = one.gathered[...].reshape(2 * HALF, 8, 128)
-    halo.drain()
+    sum_one.finish()
+    sum_one_out[...] = sum_one.gathered[...].reshape(2 * HALF, 8, 128)
     sum_one.drain()
-    sum_two.drain()
 
 
 def store_kernel(scale, response, field_grad, sum_one, sum_two, response_out, field_grad_out,

time: 58.6 us -> 53.2 us (0.908)
  Pallas kernels: 57.9 us -> 52.4 us
    pallas_call x1, Pallas kernels: 56.5 us -> 51 us  [per_device(): pl.pallas_call(step_kernel, out_shape=[near, near, sums, sums], in_specs=...]
where the time goes in v2:
time: 53.2 us; the launch traced here: 53 us
  Pallas kernels  52.4 us (98%)
  between operations  0.64 us (1%)
    pallas_call x1, Pallas kernels, per_device(): pl.pallas_call(step_kernel, out_shape=[near, near, sums, sums], in_specs=...  51 us
    pallas_call x1, Pallas kernels, per_device(): pl.pallas_call(functools.partial(store_kernel, float(samples) ** (-0.5)),...  1.42 us

profile of v2, /device:TPU:1, one launch (start us, length us, event | category | flops | bytes accessed | tf_op | source)
XLA Modules:
  0.0 53.0 jit_solution(3792653996584632011)
XLA Ops:
  0.6 51.0 %shard_map.118 = (bf16[32,64,128]{2,1,0:T(8,128)(2,1)S(1)}, bf16[32,64,128]{2,1,0:T(8,128)(2,1)S(1)}, bf16[160,8,128]{2,1,0:T(8,128)(2,1)S(1)}, bf16[160,8,128]{2,1,0:T(8,128)(2,1)S(1)}) custom-call(s32[2,4]{1,0:T(2,128)} %bitcast.15, bf16[32,64,128]{2,1,0:T(8,128)(2,1)} %bitcast.13, bf16[32,64,128]{2,1,0:T(8,128)(2,1)} %bitcast.14, ...), custom_call_target="tpu_custom_call" | custom-call | tf_op jit(solution)/shard_map/pallas_call | solution.py:751
  51.6 1.4 %shard_map.119 = (bf16[32,64,128]{2,1,0:T(8,128)(2,1)}, bf16[32,64,128]{2,1,0:T(8,128)(2,1)}, f32[144,8,128]{2,1,0:T(8,128)}, f32[1,128]{1,0:T(1,128)}, f32[144,8,128]{2,1,0:T(8,128)}, /*index=5*/f32[1,128]{1,0:T(1,128)}) custom-call(bf16[32,64,128]{2,1,0:T(8,128)(2,1)S(1)} %get-tuple-element.16.response, ...), custom_call_target="tpu_custom_call" | custom-call | tf_op jit(solution)/shard_map/pallas_call | solution.py:777

commit v3 on v2

--- a/solution.py
+++ b/solution.py
@@ -266,16 +266,6 @@
         here = lane + block * 128
         t.pick[:, block * 128 : (block + 1) * 128] = ones_where(here == pixel)
         t.border[:, block * 128 : (block + 1) * 128] = ones_where(here == plain)
-    lane_side, lane_place = facing(edge_map, lane)
-    lane_pixel = border_pixel(lane_side, lane_place)
-    lane_plain = border_pixel(lane >> 5, lane & 31)
-    for block in range(8):
-        here = row + block * 128
-        rows = slice(block * 128, (block + 1) * 128)
-        t.put_in[rows, :] = ones_where(here == lane_pixel)
-        marks = ones_where(here == lane_plain)
-        t.put[rows, 0:128] = marks
-        t.put[rows, 128:256] = marks
     cross = dot_nt(t.border[...], t.border[...]).astype(BF16)
     t.cross[:, 0:128] = cross
     t.cross[:, 128:256] = cross
@@ -304,29 +294,36 @@
     before = jnp.where(col == 0, 0.0, pltpu.roll(value, 1, 0))
     after = jnp.where(col == 31, 0.0, pltpu.roll(value, 63, 0))
     for tap, part in enumerate((before, value, after)):
-        target[frame, pl.ds(1 + 2 * pair, 2), :, tap * 128 : (tap + 1) * 128] = part.astype(
-            BF16
-        ).reshape(2, 32, 128)
+        target[tap, frame, pl.ds(1 + 2 * pair, 2)] = part.astype(BF16).reshape(2, 32, 128)
 
 
 def lay_rows(target, frame, pair, value):
     part = value.reshape(2, 32, 128)
     for tap in range(3):
-        target[frame, pl.ds(2 * pair + tap, 2), :, tap * 128 : (tap + 1) * 128] = part
+        target[tap, frame, pl.ds(2 * pair + tap, 2)] = part
 
 
 def clear_rims(shifted):
-    for frame in range(2):
-        shifted[frame, 0] = jnp.zeros((32, 384), BF16)
-        shifted[frame, 33] = jnp.zeros((32, 384), BF16)
-        shifted[frame, 34] = jnp.zeros((32, 384), BF16)
+    for tap in range(3):
+        for frame in range(2):
+            shifted[tap, frame, 0] = jnp.zeros((32, 128), BF16)
+            shifted[tap, frame, 33] = jnp.zeros((32, 128), BF16)
+            shifted[tap, frame, 34] = jnp.zeros((32, 128), BF16)
 
 
 def tile_conv(shifted, weights, result):
     for frame in range(2):
         total = None
         for row in range(4):
-            rows = shifted[frame, row : row + 32].reshape(16, 2, 32, 384)[:, 0].reshape(512, 384)
+            rows = jnp.concatenate(
+                [
+                    shifted[tap, frame, row : row + 32]
+                    .reshape(16, 2, 32, 128)[:, 0]
+                    .reshape(512, 128)
+                    for tap in range(3)
+                ],
+                axis=1,
+            )
             part = dot(rows, weights[row])
             total = part if total is None else total + part
         for pair in range(16):
@@ -339,9 +336,8 @@
 def transpose_shifted(shifted, target):
     for frame in range(2):
         for tap in range(3):
-            lanes = slice(tap * 128, (tap + 1) * 128)
-            target[lanes, frame * 1024 : (frame + 1) * 1024] = (
-                shifted[frame, 1:33, :, lanes].reshape(1024, 128).T
+            target[tap * 128 : (tap + 1) * 128, frame * 1024 : (frame + 1) * 1024] = (
+                shifted[tap, frame, 1:33].reshape(1024, 128).T
             )
 
 
@@ -388,27 +384,26 @@
     leaving[...] = dot(t.ring_back[...], split_float(stacked)).astype(BF16).reshape(4, 32, 256)
 
 
-def kernel_gradient(turned, spread_rows, ring_rows, border_rows, bias, block, own):
+def kernel_gradient(turned, spread_rows, ring_rows, border_rows, bias, own):
     total = None
     for frame in range(2):
         part = dot(
             turned[:, frame * 1024 : (frame + 1) * 1024],
-            spread_rows[frame, 1:33].reshape(1024, 384),
+            jnp.concatenate(
+                [spread_rows[tap, frame, 1:33].reshape(1024, 128) for tap in range(3)], axis=1
+            ),
         )
         total = part if total is None else total + part
-    block[...] = total
-    for side in range(4):
-        part = dot_tn(ring_rows[side], border_rows[side])
-        for tap in range(3):
-            row, col = side_tap(side, tap)
-            at = (slice(col * 128, (col + 1) * 128), slice(row * 128, (row + 1) * 128))
-            block[at] += part[tap * 128 : (tap + 1) * 128]
+    parts = [dot_tn(ring_rows[side], border_rows[side]) for side in range(4)]
     for row in range(3):
         for col in range(3):
+            value = total[col * 128 : (col + 1) * 128, row * 128 : (row + 1) * 128]
+            for side in range(4):
+                for tap in range(3):
+                    if side_tap(side, tap) == (row, col):
+                        value = value + parts[side][tap * 128 : (tap + 1) * 128]
             first = (row * 3 + col) * 16
-            own[first : first + 16] = block[
-                col * 128 : (col + 1) * 128, row * 128 : (row + 1) * 128
-            ].reshape(16, 8, 128)
+            own[first : first + 16] = value.reshape(16, 8, 128)
     own[144] = jnp.concatenate([bias, jnp.zeros((7, 128), F32)], axis=0)
     own[145:160] = jnp.zeros((15, 8, 128), F32)
 
@@ -455,8 +450,6 @@
 TABLES = {
     "pick": (128, 1024),
     "border": (128, 1024),
-    "put_in": (1024, 128),
-    "put": (1024, 256),
     "turn": (128, 128),
     "cross": (128, 256),
     "cross_in": (128, 128),
@@ -464,7 +457,7 @@
     "ring_back": (128, 768),
 }
 IMAGE = (32, 64, 128)
-SHIFTED = (2, 36, 32, 384)
+SHIFTED = (3, 2, 36, 32, 128)
 BUFFERS = {
     "source": (IMAGE, BF16),
     "upstream": (IMAGE, BF16),
@@ -477,21 +470,18 @@
     "shift_one": (SHIFTED, BF16),
     "shift_two": (SHIFTED, BF16),
     "shift_grad": (SHIFTED, BF16),
-    "row_grad": ((2, 34, 32, 384), BF16),
+    "row_grad": ((3, 2, 34, 32, 128), BF16),
     "turned_one": ((384, 2048), BF16),
     "turned_two": ((384, 2048), BF16),
     "hidden": ((2048, 128), F32),
     "hidden_border": ((128, 256), F32),
     "slope_border": ((128, 256), F32),
     "upstream_border": ((128, 256), BF16),
-    "both": ((256, 256), BF16),
     "grad": (IMAGE, BF16),
-    "share": ((16, 64, 256), F32),
     "slope": (IMAGE, F32),
     "ring_one": ((4, 64, 384), BF16),
     "ring_two": ((4, 64, 384), BF16),
     "border_grad": ((4, 64, 128), BF16),
-    "block": ((384, 384), F32),
     "leaving": ((4, 4, 32, 256), BF16),
     "arrived": ((4, 4, 32, 256), BF16),
 }
@@ -545,6 +535,16 @@
     return jnp.concatenate(frames, axis=1)
 
 
+def set_border(image, border):
+    for frame in range(2):
+        first = frame * 1024
+        part = border[:, frame * 128 : (frame + 1) * 128]
+        image[first : first + 32, :] = part[0:32]
+        image[pl.ds(first + 31, 32, stride=32), :] = part[32:64]
+        image[first + 992 : first + 1024, :] = part[64:96]
+        image[pl.ds(first, 32, stride=32), :] = part[96:128]
+
+
 def each_pair(body, start=0):
     def step(pair, carry):
         for frame in range(2):
@@ -568,7 +568,7 @@
     sum_one, sum_two = GradientSum(scratch[:count]), GradientSum(scratch[count:])
 
     mate, plane, column = sum_partners()
-    partners = [*halo_partners(), mate, *plane, *column]
+    partners = [*column, *halo_partners(), *plane, mate]
     barrier = pltpu.get_barrier_semaphore()
     for device in partners:
         pl.semaphore_signal(
@@ -591,8 +591,8 @@
     for shifted in (v.shift_one, v.shift_two, v.shift_grad):
         clear_rims(shifted)
     for frame in range(2):
-        v.row_grad[frame, 32:34, :, 0:128] = jnp.zeros((2, 32, 128), BF16)
-        v.row_grad[frame, 0:2, :, 256:384] = jnp.zeros((2, 32, 128), BF16)
+        v.row_grad[0, frame, 32:34] = jnp.zeros((2, 32, 128), BF16)
+        v.row_grad[2, frame, 0:2] = jnp.zeros((2, 32, 128), BF16)
 
     def shift_source(frame, pair, index, lanes, carry):
         lay_shifted(v.shift_one, frame, pair, v.source[index].astype(F32))
@@ -602,7 +602,7 @@
     loads[1].wait()
     lay_weights(v.first_fwd, lambda row, col: v.first[row, col])
     tile_conv(v.shift_one, v.first_fwd, v.hidden)
-    v.hidden_border[...] = border_of(v.hidden) + twice(b_first[...])
+    v.hidden_border[...] = border_of(v.hidden)
     loads[2].wait()
     lay_weights(v.second_fwd, lambda row, col: v.second[row, col])
     loads[3].wait()
@@ -613,15 +613,16 @@
 
     halo.wait(0)
     both = halo_share(tables, v.arrived.at[0], v.first, v.ring_one)
-    v.both[...] = both
-    value, slope = gelu_parts(v.hidden_border[...] + dot(tables.cross[...], both))
+    border = v.hidden_border[...] + dot(tables.cross[...], both)
+    v.hidden_border[...] = border
+    value, slope = gelu_parts(border + twice(b_first[...]))
     v.leaving[1] = dot(tables.turn[...], value.astype(BF16)).astype(BF16).reshape(4, 32, 256)
     v.slope_border[...] = slope
     halo.start(1)
-    v.share[...] = dot(tables.put[...], v.both[...]).reshape(16, 64, 256)
+    set_border(v.hidden, v.hidden_border[...])
 
     def activate(frame, pair, index, lanes, carry):
-        hidden = v.hidden[rows_of(index)] + v.share[pair, :, lanes] + b_first[...]
+        hidden = v.hidden[rows_of(index)] + b_first[...]
         value, slope = gelu_parts(hidden)
         v.slope[index] = slope
         lay_shifted(v.shift_two, frame, pair, value)
@@ -629,21 +630,22 @@
 
     each_pair(activate)
     tile_conv(v.shift_two, v.second_fwd, v.hidden)
-    v.hidden_border[...] = border_of(v.hidden) + twice(b_second[...])
+    v.hidden_border[...] = border_of(v.hidden)
     transpose_shifted(v.shift_two, v.turned_two)
 
     halo.wait(1)
     both = halo_share(tables, v.arrived.at[1], v.second, v.ring_two)
-    v.both[...] = both
-    value, slope = gelu_parts(v.hidden_border[...] + dot(tables.cross[...], both))
+    border = v.hidden_border[...] + dot(tables.cross[...], both)
+    v.hidden_border[...] = border
+    value, slope = gelu_parts(border + twice(b_second[...]))
     border = (v.upstream_border[...].astype(F32) * slope).astype(BF16)
     lay_border(border, v.border_grad)
     ring_gradient(tables, v.second, v.border_grad, v.leaving.at[2])
     halo.start(2)
-    v.share[...] = dot(tables.put[...], v.both[...]).reshape(16, 64, 256)
+    set_border(v.hidden, v.hidden_border[...])
 
     def respond(frame, pair, index, lanes, carry):
-        hidden = v.hidden[rows_of(index)] + v.share[pair, :, lanes] + b_second[...]
+        hidden = v.hidden[rows_of(index)] + b_second[...]
         value, slope = gelu_parts(hidden)
         response_out[index] = value.astype(BF16)
         grad = (v.upstream[index].astype(F32) * slope).astype(BF16)
@@ -657,7 +659,7 @@
     tile_conv(v.shift_grad, v.second_back, v.hidden)
     v.hidden_border[...] = border_of(v.hidden)
     kernel_gradient(
-        v.turned_two, v.row_grad, v.ring_two, v.border_grad, bias, v.block, sum_two.own
+        v.turned_two, v.row_grad, v.ring_two, v.border_grad, bias, sum_two.own
     )
     sum_two.start()
 
@@ -666,13 +668,12 @@
     halo.wait(2)
     came = v.arrived[2].reshape(128, 256)
     border = v.hidden_border[...] + dot(tables.cross_in[...], came)
+    set_border(v.hidden, border)
     border = (border * v.slope_border[...]).astype(BF16)
     lay_border(border, v.border_grad)
-    v.share[...] = dot(tables.put_in[...], came).reshape(16, 64, 256)
 
     def descend(frame, pair, index, lanes, carry):
-        grad = v.hidden[rows_of(index)] + v.share[pair, :, lanes]
-        grad = (grad * v.slope[index]).astype(BF16)
+        grad = (v.hidden[rows_of(index)] * v.slope[index]).astype(BF16)
         v.grad[index] = grad
         lay_rows(v.row_grad, frame, pair, grad)
         return carry + fold_rows(grad.astype(F32))
@@ -680,7 +681,7 @@
     bias = each_pair(descend, jnp.zeros((8, 128), F32))
     bias = jnp.sum(bias, axis=0, keepdims=True)
     kernel_gradient(
-        v.turned_one, v.row_grad, v.ring_one, v.border_grad, bias, v.block, sum_one.own
+        v.turned_one, v.row_grad, v.ring_one, v.border_grad, bias, sum_one.own
     )
     sum_one.start()
     ring_gradient(tables, v.first, v.border_grad, v.leaving.at[3])
@@ -694,12 +695,14 @@
     each_pair(shift_grad)
     sum_two.spread_column()
     tile_conv(v.shift_grad, v.first_back, v.hidden)
+    v.hidden_border[...] = border_of(v.hidden)
     halo.wait(3)
-    v.share[...] = dot(tables.put_in[...], v.arrived[3].reshape(128, 256)).reshape(16, 64, 256)
+    came = v.arrived[3].reshape(128, 256)
+    set_border(v.hidden, v.hidden_border[...] + dot(tables.cross_in[...], came))
     sum_one.spread_column()
 
     def finish(frame, pair, index, lanes, carry):
-        field_grad_out[index] = (v.hidden[rows_of(index)] + v.share[pair, :, lanes]).astype(BF16)
+        field_grad_out[index] = v.hidden[rows_of(index)].astype(BF16)
         return carry
 
     each_pair(finish)

time: 53.2 us -> 52.6 us (0.989)
    pallas_call x1, Pallas kernels: 51 us -> 50.4 us  [per_device(): pl.pallas_call(step_kernel, out_shape=[near, near, sums, sums], in_specs=...]
where the time goes in v3:
time: 52.6 us; the launch traced here: 52.5 us
  Pallas kernels  51.9 us (99%)
  between operations  0.64 us (1%)
    pallas_call x1, Pallas kernels, per_device(): pl.pallas_call(step_kernel, out_shape=[near, near, sums, sums], in_specs=...  50.4 us
    pallas_call x1, Pallas kernels, per_device(): pl.pallas_call(functools.partial(store_kernel, float(samples) ** (-0.5)),...  1.42 us

profile of v3, /device:TPU:1, one launch (start us, length us, event | category | flops | bytes accessed | tf_op | source)
XLA Modules:
  0.0 52.5 jit_solution(1997963168961341776)
XLA Ops:
  0.6 50.4 %shard_map.118 = (bf16[32,64,128]{2,1,0:T(8,128)(2,1)S(1)}, bf16[32,64,128]{2,1,0:T(8,128)(2,1)S(1)}, bf16[160,8,128]{2,1,0:T(8,128)(2,1)S(1)}, bf16[160,8,128]{2,1,0:T(8,128)(2,1)S(1)}) custom-call(s32[2,4]{1,0:T(2,128)} %bitcast.15, bf16[32,64,128]{2,1,0:T(8,128)(2,1)} %bitcast.13, bf16[32,64,128]{2,1,0:T(8,128)(2,1)} %bitcast.14, ...), custom_call_target="tpu_custom_call" | custom-call | tf_op jit(solution)/shard_map/pallas_call | solution.py:754
  51.1 1.4 %shard_map.119 = (bf16[32,64,128]{2,1,0:T(8,128)(2,1)}, bf16[32,64,128]{2,1,0:T(8,128)(2,1)}, f32[144,8,128]{2,1,0:T(8,128)}, f32[1,128]{1,0:T(1,128)}, f32[144,8,128]{2,1,0:T(8,128)}, /*index=5*/f32[1,128]{1,0:T(1,128)}) custom-call(bf16[32,64,128]{2,1,0:T(8,128)(2,1)S(1)} %get-tuple-element.16.response, ...), custom_call_target="tpu_custom_call" | custom-call | tf_op jit(solution)/shard_map/pallas_call | solution.py:780

commit v4 on v3

--- a/solution.py
+++ b/solution.py
@@ -14,6 +14,7 @@
 F32 = jnp.float32
 
 PLANE = 16
+SIDE = 4
 DEPTH = 8
 PIECE = 5
 HALF = PLANE * PIECE
@@ -29,16 +30,31 @@
     return tile, member, core, spot, floor
 
 
+def ring_hops(step, size):
+    return min(step, size - step)
+
+
+PLANE_STEPS = sorted(
+    [(dx, dy) for dx in range(SIDE) for dy in range(SIDE) if (dx, dy) != (0, 0)],
+    key=lambda step: -sum(ring_hops(part, SIDE) for part in step),
+)
+COLUMN_STEPS = sorted(range(1, DEPTH), key=lambda step: -ring_hops(step, DEPTH))
+
+
+def moved(spot, step):
+    across = lax.rem(spot // SIDE + step[0] + SIDE, SIDE)
+    return across * SIDE + lax.rem(lax.rem(spot, SIDE) + step[1] + SIDE, SIDE)
+
+
 def sum_partners():
     tile, member, core, spot, floor = coordinates()
     mate = (tile - core + (1 - core), member)
     plane = [
-        ((floor * PLANE + lax.rem(spot + step, PLANE)) * 2 + core, member)
-        for step in range(1, PLANE)
+        ((floor * PLANE + moved(spot, step)) * 2 + core, member) for step in PLANE_STEPS
     ]
     level = floor * 2 + member
     column = []
-    for step in range(1, DEPTH):
+    for step in COLUMN_STEPS:
         other = lax.rem(level + step, DEPTH)
         column.append((((other // 2) * PLANE + spot) * 2 + core, lax.rem(other, 2)))
     return mate, plane, column
@@ -104,32 +120,32 @@
             self.mate,
         )
 
-    def to_plane(self, step):
-        target = lax.rem(self.spot + step, PLANE)
+    def to_plane(self, index):
+        target = moved(self.spot, PLANE_STEPS[index])
         return remote(
             self.pieces.at[target],
             self.from_plane.at[self.spot],
             self.plane_sem.at[0],
             self.plane_sem.at[1],
-            self.plane[step - 1],
+            self.plane[index],
         )
 
-    def to_column(self, step):
+    def to_column(self, index):
         return remote(
             self.from_column.at[self.level],
             self.from_column.at[self.level],
             self.column_sem.at[0],
             self.column_sem.at[1],
-            self.column[step - 1],
+            self.column[index],
         )
 
-    def to_gather(self, step):
+    def to_gather(self, index):
         return remote(
             self.gathered.at[self.core, self.spot],
             self.gathered.at[self.core, self.spot],
             self.gather_sem.at[0],
             self.gather_sem.at[1],
-            self.plane[step - 1],
+            self.plane[index],
         )
 
     def to_forward(self):
@@ -156,18 +172,18 @@
         total = total.reshape(PLANE, PIECE, 8, 128)
         self.total[...] = total
         self.pieces[...] = total.astype(jnp.bfloat16)
-        for step in range(1, PLANE):
-            self.to_plane(step).start()
+        for index in range(PLANE - 1):
+            self.to_plane(index).start()
 
     def spread_column(self):
         value = self.total[self.spot]
         self.wait_all(self.from_plane, PLANE - 1, self.plane_sem.at[1])
-        for step in range(1, PLANE):
-            origin = lax.rem(self.spot + PLANE - step, PLANE)
+        for step in PLANE_STEPS:
+            origin = moved(self.spot, step)
             value = value + self.from_plane[origin].astype(jnp.float32)
         self.from_column[self.level] = value.astype(jnp.bfloat16)
-        for step in range(1, DEPTH):
-            self.to_column(step).start()
+        for index in range(DEPTH - 1):
+            self.to_column(index).start()
 
     def gather_plane(self):
         self.wait_all(self.from_column, DEPTH - 1, self.column_sem.at[1])
@@ -175,8 +191,8 @@
         for level in range(DEPTH):
             value = value + self.from_column[level].astype(jnp.float32)
         self.gathered[self.core, self.spot] = value.astype(jnp.bfloat16)
-        for step in range(1, PLANE):
-            self.to_gather(step).start()
+        for index in range(PLANE - 1):
+            self.to_gather(index).start()
 
     def forward(self):
         self.wait_all(self.gathered.at[self.core], PLANE - 1, self.gather_sem.at[1])
@@ -696,10 +712,10 @@
     sum_two.spread_column()
     tile_conv(v.shift_grad, v.first_back, v.hidden)
     v.hidden_border[...] = border_of(v.hidden)
+    sum_one.spread_column()
     halo.wait(3)
     came = v.arrived[3].reshape(128, 256)
     set_border(v.hidden, v.hidden_border[...] + dot(tables.cross_in[...], came))
-    sum_one.spread_column()
 
     def finish(frame, pair, index, lanes, carry):
         field_grad_out[index] = v.hidden[rows_of(index)].astype(BF16)

time: 52.6 us -> 51.6 us (0.981)
  Pallas kernels: 51.9 us -> 50.8 us
    pallas_call x1, Pallas kernels: 50.4 us -> 49.4 us  [per_device(): pl.pallas_call(step_kernel, out_shape=[near, near, sums, sums], in_specs=...]
where the time goes in v4:
time: 51.6 us; the launch traced here: 51.4 us
  Pallas kernels  50.8 us (98%)
  between operations  0.64 us (1%)
    pallas_call x1, Pallas kernels, per_device(): pl.pallas_call(step_kernel, out_shape=[near, near, sums, sums], in_specs=...  49.4 us
    pallas_call x1, Pallas kernels, per_device(): pl.pallas_call(functools.partial(store_kernel, float(samples) ** (-0.5)),...  1.42 us

profile of v4, /device:TPU:1, one launch (start us, length us, event | category | flops | bytes accessed | tf_op | source)
XLA Modules:
  0.0 51.4 jit_solution(17989701294849014161)
XLA Ops:
  0.6 49.4 %shard_map.118 = (bf16[32,64,128]{2,1,0:T(8,128)(2,1)S(1)}, bf16[32,64,128]{2,1,0:T(8,128)(2,1)S(1)}, bf16[160,8,128]{2,1,0:T(8,128)(2,1)S(1)}, bf16[160,8,128]{2,1,0:T(8,128)(2,1)S(1)}) custom-call(s32[2,4]{1,0:T(2,128)} %bitcast.15, bf16[32,64,128]{2,1,0:T(8,128)(2,1)} %bitcast.13, bf16[32,64,128]{2,1,0:T(8,128)(2,1)} %bitcast.14, ...), custom_call_target="tpu_custom_call" | custom-call | tf_op jit(solution)/shard_map/pallas_call | solution.py:770
  50.0 1.4 %shard_map.119 = (bf16[32,64,128]{2,1,0:T(8,128)(2,1)}, bf16[32,64,128]{2,1,0:T(8,128)(2,1)}, f32[144,8,128]{2,1,0:T(8,128)}, f32[1,128]{1,0:T(1,128)}, f32[144,8,128]{2,1,0:T(8,128)}, /*index=5*/f32[1,128]{1,0:T(1,128)}) custom-call(bf16[32,64,128]{2,1,0:T(8,128)(2,1)S(1)} %get-tuple-element.16.response, ...), custom_call_target="tpu_custom_call" | custom-call | tf_op jit(solution)/shard_map/pallas_call | solution.py:796

commit v5 on v4

--- a/solution.py
+++ b/solution.py
@@ -400,7 +400,12 @@
     leaving[...] = dot(t.ring_back[...], split_float(stacked)).astype(BF16).reshape(4, 32, 256)
 
 
-def kernel_gradient(turned, spread_rows, ring_rows, border_rows, bias, own):
+def turn_ring(ring_rows, ring_turned):
+    for side in range(4):
+        ring_turned[side] = ring_rows[side].T
+
+
+def kernel_gradient(turned, spread_rows, ring_turned, border_rows, bias, own):
     total = None
     for frame in range(2):
         part = dot(
@@ -410,7 +415,7 @@
             ),
         )
         total = part if total is None else total + part
-    parts = [dot_tn(ring_rows[side], border_rows[side]) for side in range(4)]
+    parts = [dot(ring_turned[side], border_rows[side]) for side in range(4)]
     for row in range(3):
         for col in range(3):
             value = total[col * 128 : (col + 1) * 128, row * 128 : (row + 1) * 128]
@@ -446,7 +451,7 @@
                 self.recv_sem.at[turn, (way + 2) % 4],
                 self.partners[way],
             )
-            for way in range(4)
+            for way in (1, 3, 0, 2)
         ]
 
     def start(self, turn):
@@ -497,6 +502,8 @@
     "slope": (IMAGE, F32),
     "ring_one": ((4, 64, 384), BF16),
     "ring_two": ((4, 64, 384), BF16),
+    "ring_turned_one": ((4, 384, 64), BF16),
+    "ring_turned_two": ((4, 384, 64), BF16),
     "border_grad": ((4, 64, 128), BF16),
     "leaving": ((4, 4, 32, 256), BF16),
     "arrived": ((4, 4, 32, 256), BF16),
@@ -648,6 +655,7 @@
     tile_conv(v.shift_two, v.second_fwd, v.hidden)
     v.hidden_border[...] = border_of(v.hidden)
     transpose_shifted(v.shift_two, v.turned_two)
+    turn_ring(v.ring_one, v.ring_turned_one)
 
     halo.wait(1)
     both = halo_share(tables, v.arrived.at[1], v.second, v.ring_two)
@@ -673,9 +681,10 @@
     bias = each_pair(respond, jnp.zeros((8, 128), F32))
     bias = jnp.sum(bias, axis=0, keepdims=True)
     tile_conv(v.shift_grad, v.second_back, v.hidden)
+    turn_ring(v.ring_two, v.ring_turned_two)
     v.hidden_border[...] = border_of(v.hidden)
     kernel_gradient(
-        v.turned_two, v.row_grad, v.ring_two, v.border_grad, bias, sum_two.own
+        v.turned_two, v.row_grad, v.ring_turned_two, v.border_grad, bias, sum_two.own
     )
     sum_two.start()
 
@@ -697,7 +706,7 @@
     bias = each_pair(descend, jnp.zeros((8, 128), F32))
     bias = jnp.sum(bias, axis=0, keepdims=True)
     kernel_gradient(
-        v.turned_one, v.row_grad, v.ring_one, v.border_grad, bias, sum_one.own
+        v.turned_one, v.row_grad, v.ring_turned_one, v.border_grad, bias, sum_one.own
     )
     sum_one.start()
     ring_gradient(tables, v.first, v.border_grad, v.leaving.at[3])
@@ -730,8 +739,10 @@
     sum_two_out[...] = sum_two.gathered[...].reshape(2 * HALF, 8, 128)
     sum_two.drain()
     sum_one.forward()
-    sum_one.finish()
-    sum_one_out[...] = sum_one.gathered[...].reshape(2 * HALF, 8, 128)
+    for core in (sum_one.core, 1 - sum_one.core):
+        if core is not sum_one.core:
+            sum_one.finish()
+        sum_one_out[pl.ds(core * HALF, HALF)] = sum_one.gathered[core].reshape(HALF, 8, 128)
     sum_one.drain()
 
 

time: 51.6 us -> 51.2 us (level)
  no operation moved by 1% of the time
where the time goes in v5:
time: 51.2 us; the launch traced here: 51.1 us
  Pallas kernels  50.5 us (99%)
  between operations  0.64 us (1%)
    pallas_call x1, Pallas kernels, per_device(): pl.pallas_call(step_kernel, out_shape=[near, near, sums, sums], in_specs=...  49.1 us
    pallas_call x1, Pallas kernels, per_device(): pl.pallas_call(functools.partial(store_kernel, float(samples) ** (-0.5)),...  1.42 us

profile of v5, /device:TPU:1, one launch (start us, length us, event | category | flops | bytes accessed | tf_op | source)
XLA Modules:
  0.0 51.1 jit_solution(4029621485130507441)
XLA Ops:
  0.6 49.1 %shard_map.118 = (bf16[32,64,128]{2,1,0:T(8,128)(2,1)S(1)}, bf16[32,64,128]{2,1,0:T(8,128)(2,1)S(1)}, bf16[160,8,128]{2,1,0:T(8,128)(2,1)S(1)}, bf16[160,8,128]{2,1,0:T(8,128)(2,1)S(1)}) custom-call(s32[2,4]{1,0:T(2,128)} %bitcast.15, bf16[32,64,128]{2,1,0:T(8,128)(2,1)} %bitcast.13, bf16[32,64,128]{2,1,0:T(8,128)(2,1)} %bitcast.14, ...), custom_call_target="tpu_custom_call" | custom-call | tf_op jit(solution)/shard_map/pallas_call | solution.py:781
  49.7 1.4 %shard_map.119 = (bf16[32,64,128]{2,1,0:T(8,128)(2,1)}, bf16[32,64,128]{2,1,0:T(8,128)(2,1)}, f32[144,8,128]{2,1,0:T(8,128)}, f32[1,128]{1,0:T(1,128)}, f32[144,8,128]{2,1,0:T(8,128)}, /*index=5*/f32[1,128]{1,0:T(1,128)}) custom-call(bf16[32,64,128]{2,1,0:T(8,128)(2,1)S(1)} %get-tuple-element.16.response, ...), custom_call_target="tpu_custom_call" | custom-call | tf_op jit(solution)/shard_map/pallas_call | solution.py:807

commit v6 on v5

--- a/solution.py
+++ b/solution.py
@@ -163,7 +163,8 @@
         ).wait()
 
     def start(self):
-        self.halves[...] = self.own[...].astype(jnp.bfloat16)
+        theirs = pl.ds((1 - self.core) * HALF, HALF)
+        self.halves[theirs] = self.own[theirs].astype(jnp.bfloat16)
         self.to_mate().start()
 
     def spread_plane(self):
@@ -591,7 +592,7 @@
     sum_one, sum_two = GradientSum(scratch[:count]), GradientSum(scratch[count:])
 
     mate, plane, column = sum_partners()
-    partners = [*column, *halo_partners(), *plane, mate]
+    partners = [*halo_partners(), *column, *plane, mate]
     barrier = pltpu.get_barrier_semaphore()
     for device in partners:
         pl.semaphore_signal(

time: 51.2 us -> 51.3 us (level)
  no operation moved by 1% of the time
where the time goes in v6:
time: 51.3 us; the launch traced here: 51.2 us
  Pallas kernels  50.6 us (99%)
  between operations  0.64 us (1%)
    pallas_call x1, Pallas kernels, per_device(): pl.pallas_call(step_kernel, out_shape=[near, near, sums, sums], in_specs=...  49.1 us
    pallas_call x1, Pallas kernels, per_device(): pl.pallas_call(functools.partial(store_kernel, float(samples) ** (-0.5)),...  1.42 us

profile of v6, /device:TPU:1, one launch (start us, length us, event | category | flops | bytes accessed | tf_op | source)
XLA Modules:
  0.0 51.2 jit_solution(9477275276100215956)
XLA Ops:
  0.6 49.1 %shard_map.118 = (bf16[32,64,128]{2,1,0:T(8,128)(2,1)S(1)}, bf16[32,64,128]{2,1,0:T(8,128)(2,1)S(1)}, bf16[160,8,128]{2,1,0:T(8,128)(2,1)S(1)}, bf16[160,8,128]{2,1,0:T(8,128)(2,1)S(1)}) custom-call(s32[2,4]{1,0:T(2,128)} %bitcast.15, bf16[32,64,128]{2,1,0:T(8,128)(2,1)} %bitcast.13, bf16[32,64,128]{2,1,0:T(8,128)(2,1)} %bitcast.14, ...), custom_call_target="tpu_custom_call" | custom-call | tf_op jit(solution)/shard_map/pallas_call | solution.py:782
  49.8 1.4 %shard_map.119 = (bf16[32,64,128]{2,1,0:T(8,128)(2,1)}, bf16[32,64,128]{2,1,0:T(8,128)(2,1)}, f32[144,8,128]{2,1,0:T(8,128)}, f32[1,128]{1,0:T(1,128)}, f32[144,8,128]{2,1,0:T(8,128)}, /*index=5*/f32[1,128]{1,0:T(1,128)}) custom-call(bf16[32,64,128]{2,1,0:T(8,128)(2,1)S(1)} %get-tuple-element.16.response, ...), custom_call_target="tpu_custom_call" | custom-call | tf_op jit(solution)/shard_map/pallas_call | solution.py:808
